TPU v7x, 128 devices: a whole 4x4x4 slice. The times are simulated.
128 devices in a mesh: dp: 16 (over x, z_hi, core), head: 8 (over z_lo, y).
Axes of the slice: x: 4, y: 4, z: 4 (z_hi: 2, z_lo: 2; z = z_hi * 2 + z_lo), core: 2. Of those that a mesh axis runs over, the one named last changes fastest.
Arguments:
- latent: bfloat16 [16384, 512], P(('dp', 'head')), may hold values from -32 to 32
- out_grad: bfloat16 [16384, 16, 8, 256], P('dp', None, 'head'), may hold values from -6 to 6
- weight: float32 [512, 16, 8, 256], P(None, 'dp', 'head'), may hold values from -0.25 to 0.25
- moment_one: float32 [512, 16, 8, 256], P(None, 'dp', 'head'), may hold values from -4 to 4
- moment_two: float32 [512, 16, 8, 256], P(None, 'dp', 'head'), may hold values from 0.1 to 2
Outputs:
- latent_grad: bfloat16 [16384, 512], P(('dp', 'head'))
- new_weight: float32 [512, 16, 8, 256], P(None, 'dp', 'head')
- new_moment_one: float32 [512, 16, 8, 256], P(None, 'dp', 'head')
- new_moment_two: float32 [512, 16, 8, 256], P(None, 'dp', 'head')
All inputs are finite; a program needn't handle non-finite values.
Results may differ from a plain program's by a relative error of at most 0.014.
Values may be sent and summed in bfloat16 or wider, within the bound.
No kernel may reach another device: no remote copies, remote signals or barrier semaphores. Data moves between devices by JAX's collectives and lax.ppermute only.
A program may use at most 128 MiB of HBM per device.

v0:
```python
import math
import jax
import jax.numpy as jnp
from jax import lax
from jax.sharding import PartitionSpec as P


def sent_to_all(x, axis):
    peers = lax.axis_size(axis)
    return lax.all_to_all(jnp.broadcast_to(x[None], (peers, *x.shape)), axis, 0, 0, tiled=True)


def laid_out(tiles, dim):
    tiles = jnp.moveaxis(tiles, 0, dim)
    dims = tiles.shape
    return tiles.reshape(*dims[:dim], dims[dim] * dims[dim + 1], *dims[dim + 2 :])


def gathered_copies(x, axis, dim):
    tiles = sent_to_all(x, axis)
    return laid_out(tiles, dim)


def in_blocks(x, dim, peers):
    dims = x.shape
    tiles = x.reshape(*dims[:dim], peers, dims[dim] // peers, *dims[dim + 1 :])
    return jnp.moveaxis(tiles, dim, 0)


def summed_on_arrival(x, axis, dim):
    tiles = in_blocks(x, dim, lax.axis_size(axis))
    arrived = lax.all_to_all(tiles, axis, split_axis=0, concat_axis=0, tiled=True)
    return arrived.astype(jnp.float32).sum(axis=0)


def hadamard(length):
    row_index = jnp.arange(length, dtype=jnp.int32)[:, None]
    col_index = jnp.arange(length, dtype=jnp.int32)[None, :]
    common = jnp.bitwise_and(row_index, col_index)
    parity = jnp.zeros((length, length), jnp.int32)
    for position in range(length.bit_length()):
        parity = parity + jnp.bitwise_and(jnp.right_shift(common, position), 1)
    sign_table = 1.0 - 2.0 * jnp.bitwise_and(parity, 1).astype(jnp.float32)
    return sign_table / math.sqrt(length)


def local(latent, out_grad, weight, moment_one, moment_two):
    dp_count = lax.axis_size("dp")
    latent_width = latent.shape[1]
    rotation = hadamard(latent_width)
    gathered = gathered_copies(latent, "head", 0)
    tokens_all = gathered.shape[0] * dp_count
    weight_half = weight.astype(jnp.bfloat16)
    grads_block = out_grad
    partial_value = jnp.einsum(
        "tahc,lahc->tl",
        grads_block,
        lax.all_gather(weight_half, "dp", axis=1, tiled=True),
        preferred_element_type=jnp.float32,
    )
    latent_grad = summed_on_arrival(partial_value.astype(jnp.bfloat16), "head", 0).astype(
        jnp.bfloat16
    )
    grads_block = out_grad
    partial_value = jnp.einsum(
        "tl,tahc->alc", gathered, grads_block, preferred_element_type=jnp.float32
    )
    rotated = jnp.einsum("ml,alc->amc", rotation, partial_value)
    spread = jnp.sqrt(jnp.mean(rotated * rotated, axis=1, keepdims=True) + 1e-06)
    outgoing = jnp.clip(rotated, -2.0 * spread, 2.0 * spread).astype(jnp.bfloat16)
    received = lax.all_to_all(outgoing, "dp", split_axis=0, concat_axis=0, tiled=True)
    summed = jnp.sum(received.astype(jnp.float32), axis=0)
    gradient = jnp.dot(rotation, summed) * tokens_all ** (-0.5)
    gradient = gradient.reshape(weight.shape)
    new_moment_one = 0.9 * moment_one + 0.1 * gradient
    new_moment_two = 0.95 * moment_two + 0.05 * gradient * gradient
    update = (
        new_moment_one / (1.0 - 0.9**10) / (jnp.sqrt(new_moment_two / (1.0 - 0.95**10)) + 1e-08)
    )
    new_weight = weight - 0.001 * (update + 0.1 * weight)
    return (latent_grad, new_weight, new_moment_one, new_moment_two)


def solution(mesh):
    placed = (
        P(("dp", "head"), None),
        P("dp", None, "head", None),
        P(None, "dp", "head", None),
        P(None, "dp", "head", None),
        P(None, "dp", "head", None),
    )
    return jax.shard_map(
        local,
        mesh=mesh,
        in_specs=placed,
        out_specs=(
            P(("dp", "head"), None),
            P(None, "dp", "head", None),
            P(None, "dp", "head", None),
            P(None, "dp", "head", None),
        ),
        check_vma=False,
    )
```

profile of v0, /device:TPU:1, one launch (start us, length us, event | category | flops | bytes accessed | tf_op | source)
XLA Modules:
  0.0 149.6 jit_solution(12734567798015555913)
XLA Ops:
  7.2 0.0 all-gather.2.cloned.1.call-start
  7.2 1.8 %copy.36 = bf16[512,1,1,256]{3,0,2,1:T(8,128)(2,1)} copy(f32[512,1,1,256]{3,2,1,0:T(1,128)} %param.7) | data formatting | bytes 786432 | tf_op args[2]
  9.0 0.0 all-gather.2.cloned.1.call-update
  9.0 2.0 %broadcast_in_dim.2 = bf16[8,128,512]{2,1,0:T(8,128)(2,1)} broadcast(bf16[128,512]{1,0:T(8,128)(2,1)} %param.5), dimensions={1,2} | broadcast | bytes 1179648 | tf_op jit(solution)/shard_map/broadcast_in_dim | solution.py:10
  11.0 6.4 %all-to-all-start.1 = ((bf16[8,128,512]{2,1,0:T(8,128)(2,1)}), bf16[8,128,512]{2,1,0:T(8,128)(2,1)S(1)}, u32[]{:S(2)}, u32[]{:S(2)}) async-start(bf16[8,128,512]{2,1,0:T(8,128)(2,1)} %broadcast_in_dim.2), calls=%async_computation.1 | async-start | bytes 2097152 | tf_op jit(solution)/shard_map/all_to_all | solution.py:10
  17.4 12.3 %copy.27 = bf16[1024,16,256]{0,2,1:T(8,128)(2,1)} copy(bf16[1024,16,256]{2,1,0:T(8,128)(2,1)} %bitcast.34) | data formatting | bytes 16777216 | tf_op jit(solution)/shard_map/reshape.1
  29.7 3.7 %all-to-all-done.1 = bf16[8,128,512]{2,1,0:T(8,128)(2,1)S(1)} async-done(((bf16[8,128,512]{2,1,0:T(8,128)(2,1)}), bf16[8,128,512]{2,1,0:T(8,128)(2,1)S(1)}, u32[]{:S(2)}, u32[]{:S(2)}) %all-to-all-start.1) | async-done | bytes 1048608 | tf_op jit(solution)/shard_map/all_to_all | solution.py:10
  33.4 12.4 %multiply_reduce_fusion = (f32[16,256]{1,0:T(8,128)S(1)}, bf16[16,256,512]{2,1,0:T(8,128)(2,1)}) fusion(bf16[1024,16,256]{0,2,1:T(8,128)(2,1)} %copy.27, bf16[1024,512,1]{1,0,2:T(8,128)(2,1)S(1)} %bitcast.35), kind=kOutput, calls=%fused_computation.4 | convolution fusion | flops 6457913344 | bytes 13647872 | tf_op jit(solution)/shard_map/ml,alc->amc/dot_general | solution.py:68
  45.8 4.2 %fusion.2 = bf16[16,512,256]{1,2,0:T(8,128)(2,1)} fusion(bf16[16,256,512]{2,1,0:T(8,128)(2,1)} %get-tuple-element.18, bf16[16,256]{1,0:T(8,128)(2,1)S(1)} %get-tuple-element.16, bf16[16,256]{1,0:T(8,128)(2,1)S(1)} %get-tuple-element.15), kind=kLoop, calls=%fused_computation.5 | loop fusion | flops 4194304 | bytes 8404992 | tf_op jit(solution)/shard_map/convert_element_type | solution.py:70
  49.9 8.2 %all-to-all-start.2 = ((bf16[16,512,256]{1,2,0:T(8,128)(2,1)}), bf16[16,512,256]{1,2,0:T(8,128)(2,1)}, u32[]{:S(2)}, u32[]{:S(2)}) async-start(bf16[16,512,256]{1,2,0:T(8,128)(2,1)} %fusion.2), calls=%async_computation.2 | async-start | bytes 8388608 | tf_op jit(solution)/shard_map/all_to_all | solution.py:71
  58.1 43.2 %all-gather.2.cloned.1.call-done = bf16[512,16,1,256]{3,0,2,1:T(8,128)(2,1)} async-done(((bf16[512,1,1,256]{3,0,2,1:T(8,128)(2,1)}), bf16[512,16,1,256]{3,0,2,1:T(8,128)(2,1)}) %all-gather.2.cloned.1.call-update) | async-done | bytes 4194320 | tf_op jit(solution)/shard_map/all_gather | solution.py:58
  101.3 10.1 %bitcast_convert_fusion = bf16[1024,512]{1,0:T(8,128)(2,1)} fusion(bf16[1024,16,256]{0,2,1:T(8,128)(2,1)} %copy.27, bf16[512,16,1,256]{3,0,2,1:T(8,128)(2,1)} %all-gather.2.cloned.1.call-done), kind=kOutput, calls=%fused_computation.8 | convolution fusion | flops 4295491584 | bytes 13631488 | tf_op jit(solution)/shard_map/tahc,lahc->tl/dot_general | solution.py:55
  111.4 4.1 %all-to-all-done.2 = bf16[16,512,256]{1,2,0:T(8,128)(2,1)} async-done(((bf16[16,512,256]{1,2,0:T(8,128)(2,1)}), bf16[16,512,256]{1,2,0:T(8,128)(2,1)}, u32[]{:S(2)}, u32[]{:S(2)}) %all-to-all-start.2) | async-done | bytes 4194336 | tf_op jit(solution)/shard_map/all_to_all | solution.py:71
  115.5 10.6 %all-to-all-start = ((bf16[8,128,512]{2,1,0:T(8,128)(2,1)}), bf16[8,128,512]{2,1,0:T(8,128)(2,1)S(1)}, u32[]{:S(2)}, u32[]{:S(2)}) async-start(bf16[8,128,512]{2,1,0:T(8,128)(2,1)} %bitcast.3), calls=%async_computation | async-start | bytes 2097152 | tf_op jit(solution)/shard_map/all_to_all | solution.py:32
  126.0 2.7 %convert_reduce_fusion = bf16[512,256]{0,1:T(8,128)(2,1)S(1)} fusion(bf16[16,512,256]{1,2,0:T(8,128)(2,1)} %all-to-all-done.2), kind=kLoop, calls=%fused_computation.2 | loop fusion | flops 4063232 | bytes 4456448 | tf_op jit(solution)/shard_map/reduce_sum | solution.py:72
  128.8 0.0 copy-done
  128.8 0.0 copy-done.1
  128.8 0.0 copy-done.2
  128.8 1.7 %multiply_subtract_fusion = (f32[512,1,1,256]{3,0,2,1:T(8,128)S(1)}, f32[512,1,1,256]{3,0,2,1:T(8,128)S(1)}, f32[512,1,1,256]{3,0,2,1:T(8,128)S(1)}) fusion(f32[512,1,1,256]{3,2,1,0:T(1,128)S(1)} %copy-done, f32[512,1,1,256]{3,2,1,0:T(1,128)S(1)} %copy-done.1, f32[512,1,1,256]{3,2,1,0:T(1,128)S(1)} %copy-done.2, bf16[512,256]{0,1:T(8,128)(2,1)S(1)} %convert_reduce_fusion), kind=kOutput, calls=%fused_computation.16 | convolution fusion | flops 145489920 | bytes 3407872 | tf_op jit(solution)/shard_map/dot_general | solution.py:73
  130.5 1.3 copy.24
  131.9 1.3 copy.25
  133.2 1.3 copy.26
  134.5 7.4 %all-to-all-done = bf16[8,128,512]{2,1,0:T(8,128)(2,1)S(1)} async-done(((bf16[8,128,512]{2,1,0:T(8,128)(2,1)}), bf16[8,128,512]{2,1,0:T(8,128)(2,1)S(1)}, u32[]{:S(2)}, u32[]{:S(2)}) %all-to-all-start) | async-done | bytes 1048608 | tf_op jit(solution)/shard_map/all_to_all | solution.py:32
  141.9 0.8 reduce_sum.34
  (4 shorter events, 0.0 us)
Async XLA Ops:
  7.2 94.1 %all-gather.2.cloned.1.call-start = ((), (), s32[]{:S(2)}) async-start(), calls=%async_computation.3 | async-start | bytes 4456448 | tf_op jit(solution)/shard_map/all_gather | solution.py:58
  11.0 22.3 %all-to-all-start.1 = ((bf16[8,128,512]{2,1,0:T(8,128)(2,1)}), bf16[8,128,512]{2,1,0:T(8,128)(2,1)S(1)}, u32[]{:S(2)}, u32[]{:S(2)}) async-start(bf16[8,128,512]{2,1,0:T(8,128)(2,1)} %broadcast_in_dim.2), calls=%async_computation.1 | async-start | bytes 2097152 | tf_op jit(solution)/shard_map/all_to_all | solution.py:10
  49.9 65.5 %all-to-all-start.2 = ((bf16[16,512,256]{1,2,0:T(8,128)(2,1)}), bf16[16,512,256]{1,2,0:T(8,128)(2,1)}, u32[]{:S(2)}, u32[]{:S(2)}) async-start(bf16[16,512,256]{1,2,0:T(8,128)(2,1)} %fusion.2), calls=%async_computation.2 | async-start | bytes 8388608 | tf_op jit(solution)/shard_map/all_to_all | solution.py:71
  111.4 17.4 %copy-start = (f32[512,1,1,256]{3,2,1,0:T(1,128)S(1)}, f32[512,1,1,256]{3,2,1,0:T(1,128)}, u32[]{:S(2)}) copy-start(f32[512,1,1,256]{3,2,1,0:T(1,128)} %param.7) | copy-start | bytes 1572868
  111.4 17.4 %copy-start.1 = (f32[512,1,1,256]{3,2,1,0:T(1,128)S(1)}, f32[512,1,1,256]{3,2,1,0:T(1,128)}, u32[]{:S(2)}) copy-start(f32[512,1,1,256]{3,2,1,0:T(1,128)} %param.8) | copy-start | bytes 1572868
  111.4 17.4 %copy-start.2 = (f32[512,1,1,256]{3,2,1,0:T(1,128)S(1)}, f32[512,1,1,256]{3,2,1,0:T(1,128)}, u32[]{:S(2)}) copy-start(f32[512,1,1,256]{3,2,1,0:T(1,128)} %param.9) | copy-start | bytes 1572868
  115.5 26.4 %all-to-all-start = ((bf16[8,128,512]{2,1,0:T(8,128)(2,1)}), bf16[8,128,512]{2,1,0:T(8,128)(2,1)S(1)}, u32[]{:S(2)}, u32[]{:S(2)}) async-start(bf16[8,128,512]{2,1,0:T(8,128)(2,1)} %bitcast.3), calls=%async_computation | async-start | bytes 2097152 | tf_op jit(solution)/shard_map/all_to_all | solution.py:32
Sparse Core Ops, SparseCore 0:
  10.9 90.3 all-gather.1
where the time goes:
time: 150 us
  waiting for transfers between devices  58.3 us (39%)
  starting transfers between devices  25.1 us (17%)
  matrix products  24.1 us (16%)
  local copies, waits for them, and re-layouts  20.1 us (13%)
  between operations  14.1 us (9%)
  other arithmetic  7.77 us (5%)
    all_gather x1, waiting for transfers between devices, local(): lax.all_gather(weight_half, 'dp', axis=1, tiled=True)  43.2 us
    dot_general x1, matrix products, local(): rotated = jnp.einsum('ml,alc->amc', rotation, partial_value)  12.4 us
    another operation x1, local copies, waits for them, and re-layouts  12.3 us
    all_to_all x1, starting transfers between devices, summed_on_arrival(): lax.all_to_all(tiles, axis, split_axis=0, concat_axis=0, tiled=True)  10.6 us
    dot_general x1, matrix products, local(): jnp.einsum('tahc,lahc->tl', grads_block, lax.all_gather(weight_half, 'dp'...  10.1 us
    all_to_all x1, starting transfers between devices, local(): lax.all_to_all(outgoing, 'dp', split_axis=0, concat_axis=0, tiled=True)  8.16 us
    all_to_all x1, waiting for transfers between devices, summed_on_arrival(): lax.all_to_all(tiles, axis, split_axis=0, concat_axis=0, tiled=True)  7.4 us
    all_to_all x1, starting transfers between devices, sent_to_all(): lax.all_to_all(jnp.broadcast_to(x[None], (peers, *x.shape)), axis, 0, 0,...  6.36 us
  transfers between devices with their start and end apart: 4, of which 4 were waited for; matrix products, arithmetic and copies ran while one was open for 33% of the time, Pallas kernels for 0%

commit v1 on v0

--- a/solution.py
+++ b/solution.py
@@ -55,7 +55,9 @@
     partial_value = jnp.einsum(
         "tahc,lahc->tl",
         grads_block,
-        lax.all_gather(weight_half, "dp", axis=1, tiled=True),
+        jnp.concatenate(
+            lax.all_to_all(jnp.stack([weight_half] * lax.axis_size("dp")), "dp", 0, 0), axis=1
+        ),
         preferred_element_type=jnp.float32,
     )
     latent_grad = summed_on_arrival(partial_value.astype(jnp.bfloat16), "head", 0).astype(

time: 150 us -> 181 us (1.21)
  the two profiles are of different devices: /device:TPU:1 before, /device:TPU:68 now
where the time goes in v1:
time: 181 us; the launch traced here: 180 us
  waiting for transfers between devices  102 us (56%)
  matrix products  24.1 us (13%)
  starting transfers between devices  23.7 us (13%)
  local copies, waits for them, and re-layouts  20.6 us (11%)
  other arithmetic  9.14 us (5%)
    all_to_all x1, waiting for transfers between devices, local(): lax.all_to_all(outgoing, 'dp', split_axis=0, concat_axis=0, tiled=True)  49.1 us
    all_to_all x1, waiting for transfers between devices, local(): lax.all_to_all(jnp.stack([weight_half] * lax.axis_size('dp')), 'dp', 0, 0)  30.5 us
    all_to_all x1, waiting for transfers between devices, sent_to_all(): lax.all_to_all(jnp.broadcast_to(x[None], (peers, *x.shape)), axis, 0, 0,...  14.2 us
    dot_general x1, matrix products, local(): rotated = jnp.einsum('ml,alc->amc', rotation, partial_value)  12.3 us
    another operation x1, local copies, waits for them, and re-layouts  12.3 us
    dot_general x1, matrix products, local(): jnp.einsum('tahc,lahc->tl', grads_block, jnp.concatenate(lax.all_to_all(j...  10.1 us
    all_to_all x1, waiting for transfers between devices, summed_on_arrival(): lax.all_to_all(tiles, axis, split_axis=0, concat_axis=0, tiled=True)  7.87 us
    all_to_all x1, starting transfers between devices, local(): lax.all_to_all(outgoing, 'dp', split_axis=0, concat_axis=0, tiled=True)  7.23 us
  transfers between devices with their start and end apart: 4, of which 4 were waited for; matrix products, arithmetic and copies ran while one was open for 27% of the time, Pallas kernels for 0%

profile of v1, /device:TPU:68, one launch (start us, length us, event | category | flops | bytes accessed | tf_op | source)
XLA Modules:
  0.0 179.9 jit_solution(2255026142876569756)
XLA Ops:
  0.6 2.0 %broadcast_in_dim.2 = bf16[8,128,512]{2,1,0:T(8,128)(2,1)} broadcast(bf16[128,512]{1,0:T(8,128)(2,1)} %param.5), dimensions={1,2} | broadcast | bytes 1179648 | tf_op jit(solution)/shard_map/broadcast_in_dim | solution.py:10
  2.6 5.5 %all-to-all-start.2 = ((bf16[8,128,512]{2,1,0:T(8,128)(2,1)}), bf16[8,128,512]{2,1,0:T(8,128)(2,1)S(1)}, u32[]{:S(2)}, u32[]{:S(2)}) async-start(bf16[8,128,512]{2,1,0:T(8,128)(2,1)} %broadcast_in_dim.2), calls=%async_computation.2 | async-start | bytes 2097152 | tf_op jit(solution)/shard_map/all_to_all | solution.py:10
  8.1 1.4 convert_element_type.25
  9.6 14.2 %all-to-all-done.2 = bf16[8,128,512]{2,1,0:T(8,128)(2,1)S(1)} async-done(((bf16[8,128,512]{2,1,0:T(8,128)(2,1)}), bf16[8,128,512]{2,1,0:T(8,128)(2,1)S(1)}, u32[]{:S(2)}, u32[]{:S(2)}) %all-to-all-start.2) | async-done | bytes 1048608 | tf_op jit(solution)/shard_map/all_to_all | solution.py:10
  23.8 2.3 %stack.2 = bf16[16,512,1,1,256]{4,1,3,2,0:T(8,128)(2,1)} broadcast(bf16[512,256]{1,0:T(8,128)(2,1)S(1)} %bitcast.42), dimensions={1,4} | broadcast | bytes 4456448 | tf_op jit(solution)/shard_map/stack | solution.py:59
  26.2 7.2 %all-to-all-start = ((bf16[16,512,1,1,256]{4,1,3,2,0:T(8,128)(2,1)}), bf16[16,512,1,1,256]{4,1,3,2,0:T(8,128)(2,1)}, u32[]{:S(2)}, u32[]{:S(2)}) async-start(bf16[16,512,1,1,256]{4,1,3,2,0:T(8,128)(2,1)} %stack.2), calls=%async_computation | async-start | bytes 8388608 | tf_op jit(solution)/shard_map/all_to_all | solution.py:59
  33.4 12.3 %copy.26 = bf16[1024,16,256]{0,2,1:T(8,128)(2,1)} copy(bf16[1024,16,256]{2,1,0:T(8,128)(2,1)} %bitcast.41) | data formatting | bytes 16777216 | tf_op jit(solution)/shard_map/reshape.2
  45.6 12.3 %multiply_reduce_fusion = (f32[16,256]{1,0:T(8,128)S(1)}, bf16[16,256,512]{2,1,0:T(8,128)(2,1)}) fusion(bf16[1024,16,256]{0,2,1:T(8,128)(2,1)} %copy.26, bf16[1024,512,1]{1,0,2:T(8,128)(2,1)S(1)} %bitcast.43), kind=kOutput, calls=%fused_computation.4 | convolution fusion | flops 6457913344 | bytes 13647872 | tf_op jit(solution)/shard_map/ml,alc->amc/dot_general | solution.py:70
  57.9 4.2 %fusion.2 = bf16[16,512,256]{1,2,0:T(8,128)(2,1)} fusion(bf16[16,256,512]{2,1,0:T(8,128)(2,1)} %get-tuple-element.18, bf16[16,256]{1,0:T(8,128)(2,1)S(1)} %get-tuple-element.16, bf16[16,256]{1,0:T(8,128)(2,1)S(1)} %get-tuple-element.15), kind=kLoop, calls=%fused_computation.5 | loop fusion | flops 4194304 | bytes 8404992 | tf_op jit(solution)/shard_map/convert_element_type | solution.py:72
  62.1 30.5 %all-to-all-done = bf16[16,512,1,1,256]{4,1,3,2,0:T(8,128)(2,1)} async-done(((bf16[16,512,1,1,256]{4,1,3,2,0:T(8,128)(2,1)}), bf16[16,512,1,1,256]{4,1,3,2,0:T(8,128)(2,1)}, u32[]{:S(2)}, u32[]{:S(2)}) %all-to-all-start) | async-done | bytes 4194336 | tf_op jit(solution)/shard_map/all_to_all | solution.py:59
  92.6 7.2 %all-to-all-start.3 = ((bf16[16,512,256]{1,2,0:T(8,128)(2,1)}), bf16[16,512,256]{1,2,0:T(8,128)(2,1)}, u32[]{:S(2)}, u32[]{:S(2)}) async-start(bf16[16,512,256]{1,2,0:T(8,128)(2,1)} %fusion.2), calls=%async_computation.3 | async-start | bytes 8388608 | tf_op jit(solution)/shard_map/all_to_all | solution.py:73
  99.8 10.1 %bitcast_convert_fusion = bf16[1024,512]{1,0:T(8,128)(2,1)} fusion(bf16[1024,16,256]{0,2,1:T(8,128)(2,1)} %copy.26, bf16[16,512,1,1,256]{4,1,3,2,0:T(8,128)(2,1)} %all-to-all-done), kind=kOutput, calls=%fused_computation.8 | convolution fusion | flops 4295491584 | bytes 13631488 | tf_op jit(solution)/shard_map/tahc,lahc->tl/dot_general | solution.py:55
  109.9 49.1 %all-to-all-done.3 = bf16[16,512,256]{1,2,0:T(8,128)(2,1)} async-done(((bf16[16,512,256]{1,2,0:T(8,128)(2,1)}), bf16[16,512,256]{1,2,0:T(8,128)(2,1)}, u32[]{:S(2)}, u32[]{:S(2)}) %all-to-all-start.3) | async-done | bytes 4194336 | tf_op jit(solution)/shard_map/all_to_all | solution.py:73
  159.0 3.7 %all-to-all-start.1 = ((bf16[8,128,512]{2,1,0:T(8,128)(2,1)}), bf16[8,128,512]{2,1,0:T(8,128)(2,1)S(1)}, u32[]{:S(2)}, u32[]{:S(2)}) async-start(bf16[8,128,512]{2,1,0:T(8,128)(2,1)} %bitcast.5), calls=%async_computation.1 | async-start | bytes 2097152 | tf_op jit(solution)/shard_map/all_to_all | solution.py:32
  162.7 2.8 %convert_reduce_fusion = bf16[512,256]{0,1:T(8,128)(2,1)S(1)} fusion(bf16[16,512,256]{1,2,0:T(8,128)(2,1)} %all-to-all-done.3), kind=kLoop, calls=%fused_computation.2 | loop fusion | flops 4063232 | bytes 4456448 | tf_op jit(solution)/shard_map/reduce_sum | solution.py:74
  165.5 0.0 copy-done
  165.5 0.0 copy-done.1
  165.5 0.0 copy-done.2
  165.5 1.7 multiply_subtract_fusion
  167.2 1.3 copy.23
  168.5 1.3 copy.24
  169.9 1.3 copy.25
  171.2 7.9 %all-to-all-done.1 = bf16[8,128,512]{2,1,0:T(8,128)(2,1)S(1)} async-done(((bf16[8,128,512]{2,1,0:T(8,128)(2,1)}), bf16[8,128,512]{2,1,0:T(8,128)(2,1)S(1)}, u32[]{:S(2)}, u32[]{:S(2)}) %all-to-all-start.1) | async-done | bytes 1048608 | tf_op jit(solution)/shard_map/all_to_all | solution.py:32
  179.1 0.8 reduce_sum.34
  (5 shorter events, 0.1 us)
Async XLA Ops:
  2.6 21.2 %all-to-all-start.2 = ((bf16[8,128,512]{2,1,0:T(8,128)(2,1)}), bf16[8,128,512]{2,1,0:T(8,128)(2,1)S(1)}, u32[]{:S(2)}, u32[]{:S(2)}) async-start(bf16[8,128,512]{2,1,0:T(8,128)(2,1)} %broadcast_in_dim.2), calls=%async_computation.2 | async-start | bytes 2097152 | tf_op jit(solution)/shard_map/all_to_all | solution.py:10
  26.2 66.4 %all-to-all-start = ((bf16[16,512,1,1,256]{4,1,3,2,0:T(8,128)(2,1)}), bf16[16,512,1,1,256]{4,1,3,2,0:T(8,128)(2,1)}, u32[]{:S(2)}, u32[]{:S(2)}) async-start(bf16[16,512,1,1,256]{4,1,3,2,0:T(8,128)(2,1)} %stack.2), calls=%async_computation | async-start | bytes 8388608 | tf_op jit(solution)/shard_map/all_to_all | solution.py:59
  92.6 66.4 %all-to-all-start.3 = ((bf16[16,512,256]{1,2,0:T(8,128)(2,1)}), bf16[16,512,256]{1,2,0:T(8,128)(2,1)}, u32[]{:S(2)}, u32[]{:S(2)}) async-start(bf16[16,512,256]{1,2,0:T(8,128)(2,1)} %fusion.2), calls=%async_computation.3 | async-start | bytes 8388608 | tf_op jit(solution)/shard_map/all_to_all | solution.py:73
  109.9 55.6 %copy-start = (f32[512,1,1,256]{3,2,1,0:T(1,128)S(1)}, f32[512,1,1,256]{3,2,1,0:T(1,128)}, u32[]{:S(2)}) copy-start(f32[512,1,1,256]{3,2,1,0:T(1,128)} %param.7) | copy-start | bytes 1572868
  109.9 55.6 %copy-start.1 = (f32[512,1,1,256]{3,2,1,0:T(1,128)S(1)}, f32[512,1,1,256]{3,2,1,0:T(1,128)}, u32[]{:S(2)}) copy-start(f32[512,1,1,256]{3,2,1,0:T(1,128)} %param.8) | copy-start | bytes 1572868
  109.9 55.6 %copy-start.2 = (f32[512,1,1,256]{3,2,1,0:T(1,128)S(1)}, f32[512,1,1,256]{3,2,1,0:T(1,128)}, u32[]{:S(2)}) copy-start(f32[512,1,1,256]{3,2,1,0:T(1,128)} %param.9) | copy-start | bytes 1572868
  159.0 20.1 %all-to-all-start.1 = ((bf16[8,128,512]{2,1,0:T(8,128)(2,1)}), bf16[8,128,512]{2,1,0:T(8,128)(2,1)S(1)}, u32[]{:S(2)}, u32[]{:S(2)}) async-start(bf16[8,128,512]{2,1,0:T(8,128)(2,1)} %bitcast.5), calls=%async_computation.1 | async-start | bytes 2097152 | tf_op jit(solution)/shard_map/all_to_all | solution.py:32
